TPU v7x, 256 devices: a whole 4x4x8 slice. The times are simulated.
256 devices in a mesh: seq: 16 (over x, y), fsdp: 16 (over z, core).
Axes of the slice: x: 4, y: 4, z: 8, core: 2. Of those that a mesh axis runs over, the one named last changes fastest.
Arguments:
- patches: bfloat16 [16, 8704, 1176], P('fsdp', 'seq'), may hold values from -6 to 6
- send_slot: int32 [16, 272], P('fsdp', 'seq'), may hold values from 0 to 271, as said below
- segments: int32 [16, 272], P('fsdp'), may hold values from 0 to 33, never falling along the last dimension, each value on 1 to 24 neighbouring positions
- stem_weight: bfloat16 [3584, 1176], P('fsdp'), may hold values from -0.1875 to 0.1875
- norm_gain: bfloat16 [3584], P('fsdp'), may hold values from 0.099609375 to 1.8984375
- conv_kernel: bfloat16 [5, 3584], P(None, 'fsdp'), may hold values from -3 to 3
- cotangent: bfloat16 [16, 8704, 3584], P('fsdp', 'seq'), may hold values from -6 to 6
Outputs:
- features: bfloat16 [16, 8704, 3584], P('fsdp', 'seq')
- grad_patches: bfloat16 [16, 8704, 1176], P('fsdp', 'seq')
- grad_weight: bfloat16 [3584, 1176], P('fsdp')
- grad_channels: float32 [6, 3584], P(None, 'fsdp')
Inputs may be any that keep to these rules, and one draw needn't show every extreme that they name: `send_slot`: each row is a permutation of the packed slots. At most 2 frame slots of one device go to one device's packed slots, and every device sends exactly 2 to some device; within a row the number that device s sends to device (s + o) modulo the seq axis size depends on o alone. `segments`: ids never fall along a row; a clip holds 1 to 24 slots, one exactly 24.
All inputs are finite; a program needn't handle non-finite values.
Results may differ from a plain program's by a relative error of at most 0.0056.
Values may be sent and summed in bfloat16 or wider, within the bound.
A program may use at most 192 MiB of HBM per device.

v0:
```python
import math
import jax
import jax.numpy as jnp
from jax import lax
from jax.sharding import PartitionSpec as P

EPSILON = 1e-06


def extended_2(cells, sides, width):
    for axis, dim in sides:
        count = lax.axis_size(axis)
        ends = count - 1
        head = lax.slice_in_dim(cells, 0, width, axis=dim)
        tail = lax.slice_in_dim(cells, cells.shape[dim] - width, cells.shape[dim], axis=dim)
        cells = jnp.concatenate(
            [
                lax.ppermute(tail, axis, [(i, (i + 1) % count) for i in range(ends)]),
                cells,
                lax.ppermute(head, axis, [((i + 1) % count, i) for i in range(ends)]),
            ],
            axis=dim,
        )
    return cells


def slot_mask(segment_row, centre):
    slot_total = segment_row.shape[0]
    safe_centre = jnp.clip(centre, 0, slot_total - 1)
    columns = []
    for offset in range(5):
        neighbour = centre + (offset - 2)
        inside = (neighbour >= 0) & (neighbour < slot_total) & (centre >= 0) & (centre < slot_total)
        same_clip = segment_row[jnp.clip(neighbour, 0, slot_total - 1)] == segment_row[safe_centre]
        columns.append((inside & same_clip).astype(jnp.float32))
    return jnp.stack(columns, axis=1)


def temporal_mix(padded, clip_mask, kernel, slot_total):
    kernel_wide = kernel.astype(jnp.float32)
    result = padded[0:slot_total].astype(jnp.float32) * (
        clip_mask[:, 0][:, None, None] * kernel_wide[0][None, None, :]
    )
    for offset in range(1, 5):
        addend = padded[offset : offset + slot_total].astype(jnp.float32) * (
            clip_mask[:, offset][:, None, None] * kernel_wide[offset][None, None, :]
        )
        result = result + addend
    return result


def temporal_back(slope_padded, mask_padded, kernel, slot_total):
    kernel_wide = kernel.astype(jnp.float32)
    result = jnp.zeros((slot_total,) + slope_padded.shape[1:], jnp.float32)
    for offset in range(5):
        first_row = 4 - offset
        weights_row = (
            mask_padded[first_row : first_row + slot_total, offset][:, None, None]
            * kernel_wide[offset][None, None, :]
        )
        result = (
            result
            + slope_padded[first_row : first_row + slot_total].astype(jnp.float32) * weights_row
        )
    return result


def kernel_sums(slope_blocks, padded, clip_mask, slot_total):
    stacked = []
    for offset in range(5):
        product = jnp.sum(
            slope_blocks.astype(jnp.float32)
            * padded[offset : offset + slot_total].astype(jnp.float32),
            axis=1,
        )
        stacked.append(jnp.sum(product * clip_mask[:, offset][:, None], axis=0))
    return jnp.stack(stacked, axis=0)


def rim_rows(values, margin):
    return extended_2(values, (("seq", 0),), margin)


def shards(patches, send_slot, segments, stem_weight, norm_gain, conv_kernel, cotangent):
    seq_size = lax.axis_size("seq")
    fsdp_size = lax.axis_size("fsdp")
    seq_index = lax.axis_index("seq")
    slot_count = send_slot.shape[1]
    tokens = patches.shape[1]
    slot_rows = tokens // slot_count
    pixel_width = patches.shape[2]
    capacity = 2 * slot_count // seq_size
    destination = send_slot[0]
    owner_index = destination // slot_count
    same_owner = owner_index[:, None] == owner_index[None, :]
    earlier = destination[None, :] < destination[:, None]
    ranking = jnp.sum((same_owner & earlier).astype(jnp.int32), axis=1)
    buffer_row = owner_index * capacity + ranking
    frames = patches[0].reshape(slot_count, slot_rows, pixel_width)
    outbox = (
        jnp.zeros((seq_size * capacity, slot_rows, pixel_width), jnp.bfloat16)
        .at[buffer_row]
        .set(frames)
    )
    position = (
        jnp.full((seq_size * capacity,), -1.0, jnp.float32)
        .at[buffer_row]
        .set((destination % slot_count).astype(jnp.float32))
        .astype(jnp.bfloat16)
    )
    incoming, arrived = (
        lax.all_to_all(outbox, "seq", split_axis=0, concat_axis=0, tiled=True),
        lax.all_to_all(position, "seq", split_axis=0, concat_axis=0, tiled=True),
    )
    arrived_float = arrived.astype(jnp.float32)
    target = jnp.where(arrived_float >= 0.0, arrived_float, float(slot_count)).astype(jnp.int32)
    packed = (
        jnp.zeros((slot_count + 1, slot_rows, pixel_width), jnp.bfloat16)
        .at[target]
        .set(incoming)[:slot_count]
        .reshape(tokens, pixel_width)
    )
    weight_full, gain_low, kernel_full = (
        lax.all_gather(stem_weight, "fsdp", axis=0, tiled=True),
        lax.all_gather(norm_gain, "fsdp", axis=0, tiled=True),
        lax.all_gather(conv_kernel, "fsdp", axis=1, tiled=True),
    )
    gain_wide = gain_low.astype(jnp.float32)
    channels = weight_full.shape[0]
    stem_out = lax.dot_general(
        packed, weight_full, (((1,), (1,)), ((), ())), preferred_element_type=jnp.float32
    )
    inv_rms = lax.rsqrt(jnp.mean(stem_out * stem_out, axis=1, keepdims=True) + EPSILON)
    unit_rows = stem_out * inv_rms
    normed = (unit_rows * gain_wide).astype(jnp.bfloat16)
    segment_row = segments[0]
    centre = seq_index * slot_count + jnp.arange(slot_count, dtype=jnp.int32)
    extended = seq_index * slot_count + jnp.arange(-2, slot_count + 2, dtype=jnp.int32)
    clip_mask = slot_mask(segment_row, centre)
    mask_padded = slot_mask(segment_row, extended)
    padded = rim_rows(normed, 2 * slot_rows).reshape(slot_count + 4, slot_rows, channels)
    mixed_rows = temporal_mix(padded, clip_mask, kernel_full, slot_count).reshape(tokens, channels)
    features = (stem_out + jax.nn.silu(mixed_rows)).astype(jnp.bfloat16)
    upstream_wide = cotangent[0].astype(jnp.float32)
    gate_value = jax.nn.sigmoid(mixed_rows)
    slope_low = (upstream_wide * gate_value * (1.0 + mixed_rows * (1.0 - gate_value))).astype(
        jnp.bfloat16
    )
    slope_padded = rim_rows(slope_low, 2 * slot_rows).reshape(slot_count + 4, slot_rows, channels)
    d_normed = temporal_back(slope_padded, mask_padded, kernel_full, slot_count).reshape(
        tokens, channels
    )
    gated = d_normed * gain_wide
    d_stem = upstream_wide + inv_rms * (
        gated - unit_rows * jnp.mean(gated * unit_rows, axis=1, keepdims=True)
    )
    d_stem_low = d_stem.astype(jnp.bfloat16)
    grad_rows = jnp.dot(d_stem_low, weight_full, preferred_element_type=jnp.float32).astype(
        jnp.bfloat16
    )
    gain_part = jnp.sum(d_normed * unit_rows, axis=0)
    slope_blocks = slope_padded[2 : 2 + slot_count]
    kernel_part = kernel_sums(slope_blocks, padded, clip_mask, slot_count)
    chan_terms = jnp.concatenate([gain_part[None, :], kernel_part], axis=0).T
    weight_block = lax.dot_general(
        d_stem_low, packed, (((0,), (0,)), ((), ())), preferred_element_type=jnp.float32
    )
    grad_shard = lax.psum_scatter(
        jnp.concatenate([weight_block, chan_terms], axis=1), "fsdp", scatter_dimension=0, tiled=True
    )
    summed = lax.psum(grad_shard, "seq")
    grad_scale = 1.0 / math.sqrt(tokens * seq_size * fsdp_size)
    grad_weight = (summed[:, :pixel_width] * grad_scale).astype(jnp.bfloat16)
    grad_channels = (summed[:, pixel_width:] * grad_scale).T
    return (features[None], grad_rows[None], grad_weight, grad_channels)


def solution(mesh):
    in_specs = (
        P("fsdp", "seq", None),
        P("fsdp", "seq"),
        P("fsdp", None),
        P("fsdp", None),
        P("fsdp"),
        P(None, "fsdp"),
        P("fsdp", "seq", None),
    )
    out_specs = (P("fsdp", "seq", None), P("fsdp", "seq", None), P("fsdp", None), P(None, "fsdp"))
    return jax.shard_map(shards, mesh=mesh, in_specs=in_specs, out_specs=out_specs, check_vma=False)
```

profile of v0, /device:TPU:32, one launch (start us, length us, event | category | flops | bytes accessed | tf_op | source)
XLA Modules:
  0.0 471.1 jit_solution(15271871692152045158)
XLA Ops:
  12.2 7.0 %all-to-all-start = ((bf16[16,2,1]{1,2,0:T(2,128)(2,1)}), bf16[16,2,1]{1,2,0:T(2,128)(2,1)S(1)}, u32[]{:S(2)}, u32[]{:S(2)}) async-start(bf16[16,2,1]{1,2,0:T(2,128)(2,1)} %all_to_all.12), calls=%async_computation | async-start | bytes 16384 | tf_op jit(solution)/shard_map/all_to_all | solution.py:113
  23.0 18.3 %all-gather = bf16[16,224,5]{1,2,0:T(8,128)(2,1)S(1)} all-gather(bf16[1,224,5]{1,2,0:T(8,128)(2,1)} %bitcast.126), channel_id=1, replica_groups=mesh['seq'=16,'fsdp'=16] {'fsdp'}, dimensions={0}, use_global_device_ids=true | all-gather | bytes 38080 | tf_op jit(solution)/shard_map/all_gather | solution.py:126
  47.4 1.8 broadcast_in_dim.19
  49.2 5.8 %scatter_fusion = bf16[32,32,1176]{2,1,0:T(8,128)(2,1)} fusion(bf16[32,32,1176]{2,1,0:T(8,128)(2,1)} %broadcast_in_dim.19, s32[17]{0:T(128)S(1)} %fusion.26, bf16[17,32,1176]{2,1,0:T(8,128)(2,1)S(1)} %bitcast.120), kind=kCustom, calls=%fused_computation.11 | custom fusion | bytes 3838532 | tf_op jit(solution)/shard_map/scatter | solution.py:103
  55.0 7.3 %all-to-all-start.1 = ((bf16[32,32,1176]{2,1,0:T(8,128)(2,1)}), bf16[32,32,1176]{2,1,0:T(8,128)(2,1)}, u32[]{:S(2)}, u32[]{:S(2)}) async-start(bf16[32,32,1176]{2,1,0:T(8,128)(2,1)} %scatter_fusion), calls=%async_computation.1 | async-start | bytes 5242880 | tf_op jit(solution)/shard_map/all_to_all | solution.py:112
  63.9 24.1 %all-reduce = bf16[3584]{0:T(1024)(128)(2,1)S(1)} all-reduce(bf16[3584]{0:T(1024)(128)(2,1)S(1)} %dynamic-update-slice), channel_id=1, replica_groups=mesh['seq'=16,'fsdp'=16] {'fsdp'}, use_global_device_ids=true, to_apply=%add | all-reduce | flops 3584 | bytes 14336
  90.1 8.8 %all-to-all-done.1 = bf16[32,32,1176]{2,1,0:T(8,128)(2,1)} async-done(((bf16[32,32,1176]{2,1,0:T(8,128)(2,1)}), bf16[32,32,1176]{2,1,0:T(8,128)(2,1)}, u32[]{:S(2)}, u32[]{:S(2)}) %all-to-all-start.1) | async-done | bytes 2408480 | tf_op jit(solution)/shard_map/all_to_all | solution.py:112
  99.1 4.2 scatter_fusion.1
  103.4 8.0 %multiply_reduce_fusion.2 = (f32[544]{0:T(1024)S(1)}, f32[544,3584]{1,0:T(8,128)S(1)}) fusion(bf16[544,1176]{1,0:T(8,128)(2,1)S(1)} %bitcast.121, bf16[3584,1176]{1,0:T(8,128)(2,1)} %all-gather.3.cloned.1.call-done), kind=kOutput, calls=%fused_computation.47 | convolution fusion | flops 4589583872 | bytes 17510016 | tf_op jit(solution)/shard_map/dot_general | solution.py:130
  112.9 1.6 collective-permute-start.1
  114.5 4.8 %collective-permute-start = (bf16[64,3584]{1,0:T(8,128)(2,1)S(1)}, bf16[64,3584]{1,0:T(8,128)(2,1)S(1)}, u32[]{:S(2)}, u32[]{:S(2)}) collective-permute-start(bf16[64,3584]{1,0:T(8,128)(2,1)S(1)} %get-tuple-element.46), channel_id=1, source_target_pairs={{0,16},{16,32},{32,48},{48,64},{64,80},{80,96},{96,112},{112,128},... | collective-permute-start | bytes 1376264 | tf_op jit(solution)/shard_map/ppermute | solution.py:18
  120.2 5.8 %collective-permute-done.1 = bf16[64,3584]{1,0:T(8,128)(2,1)S(1)} collective-permute-done((bf16[64,3584]{1,0:T(8,128)(2,1)S(1)}, bf16[64,3584]{1,0:T(8,128)(2,1)S(1)}, u32[]{:S(2)}, u32[]{:S(2)}) %collective-permute-start.1) | collective-permute-done | bytes 458784 | tf_op jit(solution)/shard_map/ppermute | solution.py:20
  127.4 8.3 %convert_multiply_fusion = (f32[544,3584]{1,0:T(8,128)}, bf16[544,3584]{1,0:T(8,128)(2,1)S(1)}, f32[544,3584]{1,0:T(8,128)}) fusion(bf16[64,3584]{1,0:T(8,128)(2,1)S(1)} %collective-permute-done.1, bf16[544,3584]{1,0:T(8,128)(2,1)S(1)} %multiply_convert_fusion, bf16[1,544,3584]{2,1,0:T(8,128)(2,1)S(1)} %copy-done.5, f32[17,3584]{1,0:T(8,128)S(1)} %copy-done.7, ...), kind=kLoop, calls=%fused_computation.13 | loop fusion | flops 74088448 | bytes 29431808 | tf_op jit(solution)/shard_map/mul | solution.py:72
  135.7 1.9 copy-done.3
  138.4 5.5 %collective-permute-start.3 = (bf16[64,3584]{1,0:T(8,128)(2,1)}, bf16[64,3584]{1,0:T(8,128)(2,1)}, u32[]{:S(2)}, u32[]{:S(2)}) collective-permute-start(bf16[64,3584]{1,0:T(8,128)(2,1)} %get-tuple-element.45), channel_id=1, source_target_pairs={{0,16},{16,32},{32,48},{48,64},{64,80},{80,96},{96,112},{112,128},... | collective-permute-start | bytes 1376264 | tf_op jit(solution)/shard_map/ppermute | solution.py:18
  143.9 1.5 collective-permute-start.2
  145.4 15.1 %convert_multiply_fusion.1 = (f32[544,3584]{1,0:T(8,128)}, f32[544,3584]{1,0:T(8,128)}, f32[544,3584]{1,0:T(8,128)}, f32[544,3584]{1,0:T(8,128)}) fusion(bf16[544,3584]{1,0:T(8,128)(2,1)} %copy-done.3, bf16[64,3584]{1,0:T(8,128)(2,1)S(1)} %collective-permute-done.1, bf16[544,3584]{1,0:T(8,128)(2,1)} %copy-done.4, bf16[64,3584]{1,0:T(8,128)(2,1)S(1)} %collective-permute-done), kind=kLoop, calls=%fused_computation.14 | loop fusion | flops 35094528 | bytes 39911424 | tf_op jit(solution)/shard_map/mul | solution.py:72
  160.5 4.3 reduce_sum.133
  165.0 4.4 reduce_sum.135
  169.5 4.4 reduce_sum.137
  174.0 4.4 reduce_sum.139
  178.5 4.4 reduce_sum.141
  183.0 10.2 %fusion.9 = f32[544,3584]{1,0:T(8,128)S(1)} fusion(bf16[544,3584]{1,0:T(8,128)(2,1)} %copy-done.3, bf16[64,3584]{1,0:T(8,128)(2,1)} %collective-permute-done.3, bf16[64,3584]{1,0:T(8,128)(2,1)} %collective-permute-done.2, f32[17,3584]{1,0:T(8,128)S(1)} %get-tuple-element.56, f32[17,3584]{1,0:T(8,128)} %get-tuple-element.54, ...), kind=kLoop, calls=%fused_computation.36 | loop fusion | flops 50692096 | bytes 13834240 | tf_op jit(solution)/shard_map/add | solution.py:62
  193.3 2.1 multiply_reduce_fusion
  195.4 9.9 %fusion.6 = (bf16[544,3584]{1,0:T(8,128)(2,1)}, bf16[1,544,3584]{2,1,0:T(8,128)(2,1)}) fusion(f32[544,3584]{1,0:T(8,128)S(1)} %fusion.9, f32[544,3584]{1,0:T(8,128)S(1)} %bitcast.114, bf16[1,544,3584]{2,1,0:T(8,128)(2,1)} %param.13, f32[544]{0:T(1024)S(1)} %broadcast_multiply_fusion.10, f32[3584]{0:T(1024)S(1)} %convert_element_type.185, ...), kind=kLoop, calls=%fused_computation.33 | loop fusion | flops 27295744 | bytes 35113216 | tf_op jit(solution)/shard_map/convert_element_type | solution.py:157
  205.3 12.7 %fusion.47 = f32[3584,1176]{0,1:T(8,128)} fusion(bf16[544,3584]{1,0:T(8,128)(2,1)} %get-tuple-element.42, bf16[544,1176]{1,0:T(8,128)(2,1)S(1)} %bitcast.122), kind=kOutput, calls=%fused_computation.172 | convolution fusion | flops 4585684992 | bytes 22038016 | tf_op jit(solution)/shard_map/dot_general | solution.py:165
  218.1 11.5 %pad_maximum_fusion = f32[3584,1182]{0,1:T(8,128)} fusion(f32[3584,6]{0,1:T(8,128)S(1)} %bitcast.123, f32[3584,1176]{0,1:T(8,128)} %fusion.47), kind=kLoop, calls=%fused_computation.19 | loop fusion | flops 4236288 | bytes 33890304 | tf_op jit(solution)/shard_map/concatenate | solution.py:169
  229.6 18.8 %copy.23 = f32[3584,1182]{1,0:T(8,128)} copy(f32[3584,1182]{0,1:T(8,128)} %pad_maximum_fusion) | data formatting | bytes 33890304
  248.5 109.9 %reduce-scatter.4.cloned.1.call-done = f32[224,1182]{1,0:T(8,128)} async-done(((f32[3584,1182]{1,0:T(8,128)}), f32[224,1182]{1,0:T(8,128)}) %reduce-scatter.4.cloned.1.call-update) | async-done | bytes 1059088
  358.4 2.7 copy.24
  361.1 10.4 %fusion.16 = bf16[1,544,1176]{2,1,0:T(8,128)(2,1)} fusion(bf16[544,3584]{1,0:T(8,128)(2,1)} %get-tuple-element.42, bf16[3584,1176]{1,0:T(8,128)(2,1)} %all-gather.3.cloned.1.call-done), kind=kOutput, calls=%fused_computation.66 | convolution fusion | flops 4586324992 | bytes 13608448 | tf_op jit(solution)/shard_map/dot_general | solution.py:158
  371.5 89.3 %all-reduce.3.cloned.1.call-done = f32[224,1182]{0,1:T(8,128)} async-done(((f32[224,1182]{0,1:T(8,128)}), f32[224,1182]{0,1:T(8,128)}) %all-reduce.3.cloned.1.call-update) | async-done | bytes 1059088 | tf_op jit(solution)/shard_map/psum | solution.py:171
  (123 shorter events, 27.0 us)
Async XLA Ops:
  7.2 12.1 %copy-start = (s32[1,272]{1,0:T(1,128)S(1)}, s32[1,272]{1,0:T(1,128)}, u32[]{:S(2)}) copy-start(s32[1,272]{1,0:T(1,128)} %param.9) | copy-start | bytes 3268
  7.2 42.0 %copy-start.6 = (bf16[1,544,1176]{2,1,0:T(8,128)(2,1)S(1)}, bf16[1,544,1176]{2,1,0:T(8,128)(2,1)}, u32[]{:S(2)}) copy-start(bf16[1,544,1176]{2,1,0:T(8,128)(2,1)} %param.7) | copy-start | bytes 3838468
  7.2 96.2 %all-gather.3.cloned.1.call-start = ((), (), s32[]{:S(2)}) async-start(), calls=%async_computation.3 | async-start | bytes 9748480 | tf_op jit(solution)/shard_map/all_gather | solution.py:124
  12.2 42.8 %all-to-all-start = ((bf16[16,2,1]{1,2,0:T(2,128)(2,1)}), bf16[16,2,1]{1,2,0:T(2,128)(2,1)S(1)}, u32[]{:S(2)}, u32[]{:S(2)}) async-start(bf16[16,2,1]{1,2,0:T(2,128)(2,1)} %all_to_all.12), calls=%async_computation | async-start | bytes 16384 | tf_op jit(solution)/shard_map/all_to_all | solution.py:113
  42.2 20.2 %copy-start.12 = (u32[256]{0:T(256)S(1)}, u32[256]{0:T(256)}, u32[]{:S(2)}) copy-start(u32[256]{0:T(256)} %constant.79) | copy-start | bytes 3076
  42.2 21.5 %copy-start.11 = (bf16[224]{0:T(256)(128)(2,1)S(1)}, bf16[224]{0:T(256)(128)(2,1)}, u32[]{:S(2)}) copy-start(bf16[224]{0:T(256)(128)(2,1)} %param.11) | copy-start | bytes 1348
  55.0 43.9 %all-to-all-start.1 = ((bf16[32,32,1176]{2,1,0:T(8,128)(2,1)}), bf16[32,32,1176]{2,1,0:T(8,128)(2,1)}, u32[]{:S(2)}, u32[]{:S(2)}) async-start(bf16[32,32,1176]{2,1,0:T(8,128)(2,1)} %scatter_fusion), calls=%async_computation.1 | async-start | bytes 5242880 | tf_op jit(solution)/shard_map/all_to_all | solution.py:112
  62.3 296.1 %reduce-scatter.4.cloned.1.call-start = ((), (), s32[]{:S(2)}) async-start(), calls=%async_computation.5 | async-start | bytes 19496960
  111.4 24.2 %copy-start.2 = (f32[544,3584]{1,0:T(8,128)}, f32[544,3584]{1,0:T(8,128)S(1)}, u32[]{:S(2)}) copy-start(f32[544,3584]{1,0:T(8,128)S(1)} %get-tuple-element.69) | copy-start | bytes 23396356
  111.4 15.9 %copy-start.5 = (bf16[1,544,3584]{2,1,0:T(8,128)(2,1)S(1)}, bf16[1,544,3584]{2,1,0:T(8,128)(2,1)}, u32[]{:S(2)}) copy-start(bf16[1,544,3584]{2,1,0:T(8,128)(2,1)} %param.13) | copy-start | bytes 11698180
  111.5 15.9 %copy-start.7 = (f32[17,3584]{1,0:T(8,128)S(1)}, f32[17,3584]{1,0:T(8,128)}, u32[]{:S(2)}) copy-start(f32[17,3584]{1,0:T(8,128)} %get-tuple-element.57) | copy-start | bytes 731140
  111.5 15.9 %copy-start.8 = (f32[17,3584]{1,0:T(8,128)S(1)}, f32[17,3584]{1,0:T(8,128)}, u32[]{:S(2)}) copy-start(f32[17,3584]{1,0:T(8,128)} %get-tuple-element.55) | copy-start | bytes 731140
  111.5 15.9 %copy-start.9 = (f32[17,3584]{1,0:T(8,128)S(1)}, f32[17,3584]{1,0:T(8,128)}, u32[]{:S(2)}) copy-start(f32[17,3584]{1,0:T(8,128)} %get-tuple-element.53) | copy-start | bytes 731140
  111.5 15.9 %copy-start.10 = (f32[17,3584]{1,0:T(8,128)S(1)}, f32[17,3584]{1,0:T(8,128)}, u32[]{:S(2)}) copy-start(f32[17,3584]{1,0:T(8,128)} %get-tuple-element.51) | copy-start | bytes 731140
  112.8 22.9 %copy-start.4 = (bf16[544,3584]{1,0:T(8,128)(2,1)}, bf16[544,3584]{1,0:T(8,128)(2,1)S(1)}, u32[]{:S(2)}) copy-start(bf16[544,3584]{1,0:T(8,128)(2,1)S(1)} %multiply_convert_fusion) | copy-start | bytes 11698180
  112.9 13.1 %collective-permute-start.1 = (bf16[64,3584]{1,0:T(8,128)(2,1)S(1)}, bf16[64,3584]{1,0:T(8,128)(2,1)S(1)}, u32[]{:S(2)}, u32[]{:S(2)}) collective-permute-start(bf16[64,3584]{1,0:T(8,128)(2,1)S(1)} %get-tuple-element.47), channel_id=1, source_target_pairs={{16,0},{32,16},{48,32},{64,48},{80,64},{96,80},{112,96},{128,112},... | collective-permute-start | bytes 1376264 | tf_op jit(solution)/shard_map/ppermute | solution.py:20
  114.5 12.9 %collective-permute-start = (bf16[64,3584]{1,0:T(8,128)(2,1)S(1)}, bf16[64,3584]{1,0:T(8,128)(2,1)S(1)}, u32[]{:S(2)}, u32[]{:S(2)}) collective-permute-start(bf16[64,3584]{1,0:T(8,128)(2,1)S(1)} %get-tuple-element.46), channel_id=1, source_target_pairs={{0,16},{16,32},{32,48},{48,64},{64,80},{80,96},{96,112},{112,128},... | collective-permute-start | bytes 1376264 | tf_op jit(solution)/shard_map/ppermute | solution.py:18
  135.7 1.9 copy-start.3
  138.4 44.6 %collective-permute-start.3 = (bf16[64,3584]{1,0:T(8,128)(2,1)}, bf16[64,3584]{1,0:T(8,128)(2,1)}, u32[]{:S(2)}, u32[]{:S(2)}) collective-permute-start(bf16[64,3584]{1,0:T(8,128)(2,1)} %get-tuple-element.45), channel_id=1, source_target_pairs={{0,16},{16,32},{32,48},{48,64},{64,80},{80,96},{96,112},{112,128},... | collective-permute-start | bytes 1376264 | tf_op jit(solution)/shard_map/ppermute | solution.py:18
  143.9 39.1 %collective-permute-start.2 = (bf16[64,3584]{1,0:T(8,128)(2,1)S(1)}, bf16[64,3584]{1,0:T(8,128)(2,1)}, u32[]{:S(2)}, u32[]{:S(2)}) collective-permute-start(bf16[64,3584]{1,0:T(8,128)(2,1)S(1)} %get-tuple-element.44), channel_id=1, source_target_pairs={{16,0},{32,16},{48,32},{64,48},{80,64},{96,80},{112,96},{128,112},... | collective-permute-start | bytes 1376264 | tf_op jit(solution)/shard_map/ppermute | solution.py:20
  182.8 10.4 %slice-start = ((s8[7798784]{0:T(1024)(128)(4,1)}), s8[4194304]{0:T(1024)(128)(4,1)S(1)}, s32[]{:S(2)}) async-start(s8[7798784]{0:T(1024)(128)(4,1)} %bitcast.113), calls=%async_computation.6 | async-start | bytes 8388608
  183.0 10.3 %slice-start.1 = ((s8[7798784]{0:T(1024)(128)(4,1)}), s8[3604480]{0:T(1024)(128)(4,1)S(1)}, s32[]{:S(2)}) async-start(s8[7798784]{0:T(1024)(128)(4,1)} %bitcast.113), calls=%async_computation.7 | async-start | bytes 7208960
  248.5 212.3 %all-reduce.3.cloned.1.call-start = ((), (), s32[]{:S(2)}) async-start(), calls=%async_computation.4 | async-start | bytes 2424832 | tf_op jit(solution)/shard_map/psum | solution.py:171
  361.1 103.5 %copy-start.1 = (s32[1,272]{1,0:T(1,128)S(1)}, s32[1,272]{1,0:T(1,128)}, u32[]{:S(2)}) copy-start(s32[1,272]{1,0:T(1,128)} %param.9) | copy-start | bytes 3268
Sparse Core Ops, SparseCore 0:
  9.9 60.7 all-gather.2
  248.6 109.7 reduce-scatter.3
  361.7 99.0 all-reduce.2
where the time goes:
time: 472 us; the launch traced here: 471 us
  waiting for transfers between devices  216 us (46%)
  other arithmetic  91.6 us (19%)
  local copies, waits for them, and re-layouts  47.3 us (10%)
  blocking collectives  42.4 us (9%)
  matrix products  31.1 us (7%)
  starting transfers between devices  27.8 us (6%)
  between operations  15 us (3%)
    unnamed x4, waiting for transfers between devices  111 us
    psum x1, waiting for transfers between devices, shards(): summed = lax.psum(grad_shard, 'seq')  89.3 us
    unnamed x36, local copies, waits for them, and re-layouts  25.4 us
    unnamed x1, blocking collectives  24.1 us
    mul x2, other arithmetic, kernel_sums(): slope_blocks.astype(jnp.float32)  23.4 us
    reduce_sum x5, other arithmetic, kernel_sums(): jnp.sum(slope_blocks.astype(jnp.float32) * padded[offset:offset + slot_to...  21.8 us
    all_gather x1, blocking collectives, shards(): lax.all_gather(conv_kernel, 'fsdp', axis=1, tiled=True)  18.3 us
    dot_general x1, matrix products, shards(): lax.dot_general(d_stem_low, packed, (((0,), (0,)), ((), ())), preferred_e...  12.7 us
  transfers between devices with their start and end apart: 9, of which 5 were waited for; matrix products, arithmetic and copies ran while one was open for 16% of the time, Pallas kernels for 0%

commit v1 on v0

--- a/solution.py
+++ b/solution.py
@@ -123,7 +123,9 @@
     weight_full, gain_low, kernel_full = (
         lax.all_gather(stem_weight, "fsdp", axis=0, tiled=True),
         lax.all_gather(norm_gain, "fsdp", axis=0, tiled=True),
-        lax.all_gather(conv_kernel, "fsdp", axis=1, tiled=True),
+        jnp.concatenate(
+            lax.all_to_all(jnp.stack([conv_kernel] * lax.axis_size("fsdp")), "fsdp", 0, 0), axis=1
+        ),
     )
     gain_wide = gain_low.astype(jnp.float32)
     channels = weight_full.shape[0]

time: 472 us -> 495 us (1.049)
  waiting for transfers between devices: 216 us -> 243 us
  blocking collectives: 42.4 us -> 27.5 us
  starting transfers between devices: 27.8 us -> 35.3 us
    all_to_all x1, waiting for transfers between devices: 8.8 us -> 32.1 us  [shards(): lax.all_to_all(outbox, 'seq', split_axis=0, concat_axis=0, tiled=True)]
    all_gather x1 -> x0, blocking collectives: 18.3 us -> none  [shards(): lax.all_gather(conv_kernel, 'fsdp', axis=1, tiled=True)]
    all_to_all x0 -> x1, starting transfers between devices: none -> 7.84 us  [shards(): lax.all_to_all(jnp.stack([conv_kernel] * lax.axis_size('fsdp')), 'fsdp',...]
    all_to_all x0 -> x1, waiting for transfers between devices: none -> 6.39 us  [shards(): lax.all_to_all(jnp.stack([conv_kernel] * lax.axis_size('fsdp')), 'fsdp',...]
    unnamed x36 -> x34, local copies, waits for them, and re-layouts: 25.4 us -> 26.7 us
  transfers between devices with their start and end apart: 9 -> 10, of which waited for: 5 -> 6; matrix products, arithmetic and copies ran while one was open for 16% -> 16% of each run, Pallas kernels for 0% -> 0%
where the time goes in v1:
time: 495 us; the launch traced here: 493 us
  waiting for transfers between devices  243 us (49%)
  other arithmetic  91.6 us (19%)
  local copies, waits for them, and re-layouts  49.6 us (10%)
  starting transfers between devices  35.3 us (7%)
  matrix products  31.2 us (6%)
  blocking collectives  27.5 us (6%)
  between operations  15 us (3%)
    unnamed x4, waiting for transfers between devices  109 us
    psum x1, waiting for transfers between devices, shards(): summed = lax.psum(grad_shard, 'seq')  89.2 us
    all_to_all x1, waiting for transfers between devices, shards(): lax.all_to_all(outbox, 'seq', split_axis=0, concat_axis=0, tiled=True)  32.1 us
    unnamed x1, blocking collectives  27.5 us
    unnamed x34, local copies, waits for them, and re-layouts  26.7 us
    mul x2, other arithmetic, kernel_sums(): slope_blocks.astype(jnp.float32)  23.4 us
    reduce_sum x5, other arithmetic, kernel_sums(): jnp.sum(slope_blocks.astype(jnp.float32) * padded[offset:offset + slot_to...  21.8 us
    dot_general x1, matrix products, shards(): lax.dot_general(d_stem_low, packed, (((0,), (0,)), ((), ())), preferred_e...  12.7 us
  transfers between devices with their start and end apart: 10, of which 6 were waited for; matrix products, arithmetic and copies ran while one was open for 16% of the time, Pallas kernels for 0%

profile of v1, /device:TPU:32, one launch (start us, length us, event | category | flops | bytes accessed | tf_op | source)
XLA Modules:
  0.0 493.5 jit_solution(14948342749397299157)
XLA Ops:
  12.2 7.0 %all-to-all-start = ((bf16[16,2,1]{1,2,0:T(2,128)(2,1)}), bf16[16,2,1]{1,2,0:T(2,128)(2,1)S(1)}, u32[]{:S(2)}, u32[]{:S(2)}) async-start(bf16[16,2,1]{1,2,0:T(2,128)(2,1)} %all_to_all.16), calls=%async_computation | async-start | bytes 16384 | tf_op jit(solution)/shard_map/all_to_all | solution.py:113
  22.0 27.5 %all-reduce = bf16[3584]{0:T(1024)(128)(2,1)S(1)} all-reduce(bf16[3584]{0:T(1024)(128)(2,1)S(1)} %dynamic-update-slice), channel_id=1, replica_groups=mesh['seq'=16,'fsdp'=16] {'fsdp'}, use_global_device_ids=true, to_apply=%add | all-reduce | flops 3584 | bytes 14336
  57.3 1.8 broadcast_in_dim.19
  59.1 5.9 %scatter_fusion = bf16[32,32,1176]{2,1,0:T(8,128)(2,1)} fusion(bf16[32,32,1176]{2,1,0:T(8,128)(2,1)} %broadcast_in_dim.19, s32[17]{0:T(128)S(1)} %fusion.26, bf16[17,32,1176]{2,1,0:T(8,128)(2,1)S(1)} %bitcast.116), kind=kCustom, calls=%fused_computation.11 | custom fusion | bytes 3838532 | tf_op jit(solution)/shard_map/scatter | solution.py:103
  65.6 7.8 %all-to-all-start.2 = ((bf16[16,5,224]{2,1,0:T(8,128)(2,1)}), bf16[16,5,224]{2,1,0:T(8,128)(2,1)S(1)}, u32[]{:S(2)}, u32[]{:S(2)}) async-start(bf16[16,5,224]{2,1,0:T(8,128)(2,1)} %stack.12), calls=%async_computation.2 | async-start | bytes 131072 | tf_op jit(solution)/shard_map/all_to_all | solution.py:127
  73.6 6.4 %all-to-all-done.2 = bf16[16,5,224]{2,1,0:T(8,128)(2,1)S(1)} async-done(((bf16[16,5,224]{2,1,0:T(8,128)(2,1)}), bf16[16,5,224]{2,1,0:T(8,128)(2,1)S(1)}, u32[]{:S(2)}, u32[]{:S(2)}) %all-to-all-start.2) | async-done | bytes 35872 | tf_op jit(solution)/shard_map/all_to_all | solution.py:127
  80.0 7.3 %all-to-all-start.1 = ((bf16[32,32,1176]{2,1,0:T(8,128)(2,1)}), bf16[32,32,1176]{2,1,0:T(8,128)(2,1)}, u32[]{:S(2)}, u32[]{:S(2)}) async-start(bf16[32,32,1176]{2,1,0:T(8,128)(2,1)} %scatter_fusion), calls=%async_computation.1 | async-start | bytes 5242880 | tf_op jit(solution)/shard_map/all_to_all | solution.py:112
  91.7 32.1 %all-to-all-done.1 = bf16[32,32,1176]{2,1,0:T(8,128)(2,1)} async-done(((bf16[32,32,1176]{2,1,0:T(8,128)(2,1)}), bf16[32,32,1176]{2,1,0:T(8,128)(2,1)}, u32[]{:S(2)}, u32[]{:S(2)}) %all-to-all-start.1) | async-done | bytes 2408480 | tf_op jit(solution)/shard_map/all_to_all | solution.py:112
  124.0 4.2 scatter_fusion.1
  128.3 8.0 %multiply_reduce_fusion.2 = (f32[544]{0:T(1024)S(1)}, f32[544,3584]{1,0:T(8,128)S(1)}) fusion(bf16[544,1176]{1,0:T(8,128)(2,1)S(1)} %bitcast.117, bf16[3584,1176]{1,0:T(8,128)(2,1)} %all-gather.2.cloned.1.call-done), kind=kOutput, calls=%fused_computation.47 | convolution fusion | flops 4589583872 | bytes 17510016 | tf_op jit(solution)/shard_map/dot_general | solution.py:132
  137.8 1.6 collective-permute-start.1
  139.3 4.8 collective-permute-start
  145.1 5.7 %collective-permute-done.1 = bf16[64,3584]{1,0:T(8,128)(2,1)S(1)} collective-permute-done((bf16[64,3584]{1,0:T(8,128)(2,1)S(1)}, bf16[64,3584]{1,0:T(8,128)(2,1)S(1)}, u32[]{:S(2)}, u32[]{:S(2)}) %collective-permute-start.1) | collective-permute-done | bytes 458784 | tf_op jit(solution)/shard_map/ppermute | solution.py:20
  152.1 8.3 %convert_multiply_fusion = (f32[544,3584]{1,0:T(8,128)}, bf16[544,3584]{1,0:T(8,128)(2,1)S(1)}, f32[544,3584]{1,0:T(8,128)}) fusion(bf16[64,3584]{1,0:T(8,128)(2,1)S(1)} %collective-permute-done.1, bf16[544,3584]{1,0:T(8,128)(2,1)S(1)} %multiply_convert_fusion, bf16[1,544,3584]{2,1,0:T(8,128)(2,1)S(1)} %copy-done.5, f32[17,3584]{1,0:T(8,128)S(1)} %copy-done.7, ...), kind=kLoop, calls=%fused_computation.13 | loop fusion | flops 74088448 | bytes 29431808 | tf_op jit(solution)/shard_map/mul | solution.py:72
  160.4 1.9 copy-done.3
  163.1 5.2 %collective-permute-start.3 = (bf16[64,3584]{1,0:T(8,128)(2,1)}, bf16[64,3584]{1,0:T(8,128)(2,1)}, u32[]{:S(2)}, u32[]{:S(2)}) collective-permute-start(bf16[64,3584]{1,0:T(8,128)(2,1)} %get-tuple-element.41), channel_id=1, source_target_pairs={{0,16},{16,32},{32,48},{48,64},{64,80},{80,96},{96,112},{112,128},... | collective-permute-start | bytes 1376264 | tf_op jit(solution)/shard_map/ppermute | solution.py:18
  169.8 15.1 %convert_multiply_fusion.1 = (f32[544,3584]{1,0:T(8,128)}, f32[544,3584]{1,0:T(8,128)}, f32[544,3584]{1,0:T(8,128)}, f32[544,3584]{1,0:T(8,128)}) fusion(bf16[544,3584]{1,0:T(8,128)(2,1)} %copy-done.3, bf16[64,3584]{1,0:T(8,128)(2,1)S(1)} %collective-permute-done.1, bf16[544,3584]{1,0:T(8,128)(2,1)} %copy-done.4, bf16[64,3584]{1,0:T(8,128)(2,1)S(1)} %collective-permute-done), kind=kLoop, calls=%fused_computation.14 | loop fusion | flops 35094528 | bytes 39911424 | tf_op jit(solution)/shard_map/mul | solution.py:72
  184.9 4.3 reduce_sum.133
  189.4 4.4 reduce_sum.135
  193.9 4.4 reduce_sum.137
  198.4 4.4 reduce_sum.139
  202.9 4.4 reduce_sum.141
  207.5 10.2 %fusion.9 = f32[544,3584]{1,0:T(8,128)S(1)} fusion(bf16[544,3584]{1,0:T(8,128)(2,1)} %copy-done.3, bf16[64,3584]{1,0:T(8,128)(2,1)} %collective-permute-done.3, bf16[64,3584]{1,0:T(8,128)(2,1)} %collective-permute-done.2, f32[17,3584]{1,0:T(8,128)S(1)} %get-tuple-element.52, f32[17,3584]{1,0:T(8,128)} %get-tuple-element.50, ...), kind=kLoop, calls=%fused_computation.36 | loop fusion | flops 50692096 | bytes 13834240 | tf_op jit(solution)/shard_map/add | solution.py:62
  217.7 2.1 multiply_reduce_fusion
  219.8 9.9 %fusion.6 = (bf16[544,3584]{1,0:T(8,128)(2,1)}, bf16[1,544,3584]{2,1,0:T(8,128)(2,1)}) fusion(f32[544,3584]{1,0:T(8,128)S(1)} %fusion.9, f32[544,3584]{1,0:T(8,128)S(1)} %bitcast.110, bf16[1,544,3584]{2,1,0:T(8,128)(2,1)} %param.13, f32[544]{0:T(1024)S(1)} %broadcast_multiply_fusion.10, f32[3584]{0:T(1024)S(1)} %convert_element_type.189, ...), kind=kLoop, calls=%fused_computation.33 | loop fusion | flops 27295744 | bytes 35113216 | tf_op jit(solution)/shard_map/convert_element_type | solution.py:159
  229.7 12.7 %fusion.47 = f32[3584,1176]{0,1:T(8,128)} fusion(bf16[544,3584]{1,0:T(8,128)(2,1)} %get-tuple-element.38, bf16[544,1176]{1,0:T(8,128)(2,1)S(1)} %bitcast.118), kind=kOutput, calls=%fused_computation.172 | convolution fusion | flops 4585684992 | bytes 22038016 | tf_op jit(solution)/shard_map/dot_general | solution.py:167
  242.6 11.5 %pad_maximum_fusion = f32[3584,1182]{0,1:T(8,128)} fusion(f32[3584,6]{0,1:T(8,128)S(1)} %bitcast.119, f32[3584,1176]{0,1:T(8,128)} %fusion.47), kind=kLoop, calls=%fused_computation.19 | loop fusion | flops 4236288 | bytes 33890304 | tf_op jit(solution)/shard_map/concatenate | solution.py:171
  254.1 18.8 %copy.17 = f32[3584,1182]{1,0:T(8,128)} copy(f32[3584,1182]{0,1:T(8,128)} %pad_maximum_fusion) | data formatting | bytes 33890304
  273.0 107.9 %reduce-scatter.4.cloned.1.call-done = f32[224,1182]{1,0:T(8,128)} async-done(((f32[3584,1182]{1,0:T(8,128)}), f32[224,1182]{1,0:T(8,128)}) %reduce-scatter.4.cloned.1.call-update) | async-done | bytes 1059088
  380.8 2.7 copy.18
  383.6 10.4 %fusion.16 = bf16[1,544,1176]{2,1,0:T(8,128)(2,1)} fusion(bf16[544,3584]{1,0:T(8,128)(2,1)} %get-tuple-element.38, bf16[3584,1176]{1,0:T(8,128)(2,1)} %all-gather.2.cloned.1.call-done), kind=kOutput, calls=%fused_computation.66 | convolution fusion | flops 4586324992 | bytes 13608448 | tf_op jit(solution)/shard_map/dot_general | solution.py:160
  394.0 89.2 %all-reduce.3.cloned.1.call-done = f32[224,1182]{0,1:T(8,128)} async-done(((f32[224,1182]{0,1:T(8,128)}), f32[224,1182]{0,1:T(8,128)}) %all-reduce.3.cloned.1.call-update) | async-done | bytes 1059088 | tf_op jit(solution)/shard_map/psum | solution.py:173
  (127 shorter events, 30.7 us)
Async XLA Ops:
  7.2 42.4 %copy-start = (s32[1,272]{1,0:T(1,128)S(1)}, s32[1,272]{1,0:T(1,128)}, u32[]{:S(2)}) copy-start(s32[1,272]{1,0:T(1,128)} %param.9) | copy-start | bytes 3268
  7.2 51.9 %copy-start.6 = (bf16[1,544,1176]{2,1,0:T(8,128)(2,1)S(1)}, bf16[1,544,1176]{2,1,0:T(8,128)(2,1)}, u32[]{:S(2)}) copy-start(bf16[1,544,1176]{2,1,0:T(8,128)(2,1)} %param.7) | copy-start | bytes 3838468
  7.2 57.8 %copy-start.11 = (bf16[5,224]{1,0:T(8,128)(2,1)S(1)}, bf16[5,224]{1,0:T(8,128)(2,1)}, u32[]{:S(2)}) copy-start(bf16[5,224]{1,0:T(8,128)(2,1)} %param.12) | copy-start | bytes 6724
  7.2 121.1 %all-gather.2.cloned.1.call-start = ((), (), s32[]{:S(2)}) async-start(), calls=%async_computation.4 | async-start | bytes 9748480 | tf_op jit(solution)/shard_map/all_gather | solution.py:124
  12.2 52.8 %all-to-all-start = ((bf16[16,2,1]{1,2,0:T(2,128)(2,1)}), bf16[16,2,1]{1,2,0:T(2,128)(2,1)S(1)}, u32[]{:S(2)}, u32[]{:S(2)}) async-start(bf16[16,2,1]{1,2,0:T(2,128)(2,1)} %all_to_all.16), calls=%async_computation | async-start | bytes 16384 | tf_op jit(solution)/shard_map/all_to_all | solution.py:113
  65.6 14.4 %all-to-all-start.2 = ((bf16[16,5,224]{2,1,0:T(8,128)(2,1)}), bf16[16,5,224]{2,1,0:T(8,128)(2,1)S(1)}, u32[]{:S(2)}, u32[]{:S(2)}) async-start(bf16[16,5,224]{2,1,0:T(8,128)(2,1)} %stack.12), calls=%async_computation.2 | async-start | bytes 131072 | tf_op jit(solution)/shard_map/all_to_all | solution.py:127
  80.0 43.8 %all-to-all-start.1 = ((bf16[32,32,1176]{2,1,0:T(8,128)(2,1)}), bf16[32,32,1176]{2,1,0:T(8,128)(2,1)}, u32[]{:S(2)}, u32[]{:S(2)}) async-start(bf16[32,32,1176]{2,1,0:T(8,128)(2,1)} %scatter_fusion), calls=%async_computation.1 | async-start | bytes 5242880 | tf_op jit(solution)/shard_map/all_to_all | solution.py:112
  87.2 293.6 %reduce-scatter.4.cloned.1.call-start = ((), (), s32[]{:S(2)}) async-start(), calls=%async_computation.6 | async-start | bytes 19496960
  136.3 24.1 %copy-start.2 = (f32[544,3584]{1,0:T(8,128)}, f32[544,3584]{1,0:T(8,128)S(1)}, u32[]{:S(2)}) copy-start(f32[544,3584]{1,0:T(8,128)S(1)} %get-tuple-element.65) | copy-start | bytes 23396356
  136.3 15.7 %copy-start.5 = (bf16[1,544,3584]{2,1,0:T(8,128)(2,1)S(1)}, bf16[1,544,3584]{2,1,0:T(8,128)(2,1)}, u32[]{:S(2)}) copy-start(bf16[1,544,3584]{2,1,0:T(8,128)(2,1)} %param.13) | copy-start | bytes 11698180
  136.3 15.7 %copy-start.7 = (f32[17,3584]{1,0:T(8,128)S(1)}, f32[17,3584]{1,0:T(8,128)}, u32[]{:S(2)}) copy-start(f32[17,3584]{1,0:T(8,128)} %get-tuple-element.53) | copy-start | bytes 731140
  136.3 15.7 %copy-start.8 = (f32[17,3584]{1,0:T(8,128)S(1)}, f32[17,3584]{1,0:T(8,128)}, u32[]{:S(2)}) copy-start(f32[17,3584]{1,0:T(8,128)} %get-tuple-element.51) | copy-start | bytes 731140
  136.4 15.7 %copy-start.9 = (f32[17,3584]{1,0:T(8,128)S(1)}, f32[17,3584]{1,0:T(8,128)}, u32[]{:S(2)}) copy-start(f32[17,3584]{1,0:T(8,128)} %get-tuple-element.49) | copy-start | bytes 731140
  136.4 15.7 %copy-start.10 = (f32[17,3584]{1,0:T(8,128)S(1)}, f32[17,3584]{1,0:T(8,128)}, u32[]{:S(2)}) copy-start(f32[17,3584]{1,0:T(8,128)} %get-tuple-element.47) | copy-start | bytes 731140
  137.7 22.7 %copy-start.4 = (bf16[544,3584]{1,0:T(8,128)(2,1)}, bf16[544,3584]{1,0:T(8,128)(2,1)S(1)}, u32[]{:S(2)}) copy-start(bf16[544,3584]{1,0:T(8,128)(2,1)S(1)} %multiply_convert_fusion) | copy-start | bytes 11698180
  137.8 13.0 %collective-permute-start.1 = (bf16[64,3584]{1,0:T(8,128)(2,1)S(1)}, bf16[64,3584]{1,0:T(8,128)(2,1)S(1)}, u32[]{:S(2)}, u32[]{:S(2)}) collective-permute-start(bf16[64,3584]{1,0:T(8,128)(2,1)S(1)} %get-tuple-element.43), channel_id=1, source_target_pairs={{16,0},{32,16},{48,32},{64,48},{80,64},{96,80},{112,96},{128,112},... | collective-permute-start | bytes 1376264 | tf_op jit(solution)/shard_map/ppermute | solution.py:20
  139.3 12.7 %collective-permute-start = (bf16[64,3584]{1,0:T(8,128)(2,1)S(1)}, bf16[64,3584]{1,0:T(8,128)(2,1)S(1)}, u32[]{:S(2)}, u32[]{:S(2)}) collective-permute-start(bf16[64,3584]{1,0:T(8,128)(2,1)S(1)} %get-tuple-element.42), channel_id=1, source_target_pairs={{0,16},{16,32},{32,48},{48,64},{64,80},{80,96},{96,112},{112,128},... | collective-permute-start | bytes 1376264 | tf_op jit(solution)/shard_map/ppermute | solution.py:18
  160.4 1.9 copy-start.3
  163.1 44.3 %collective-permute-start.3 = (bf16[64,3584]{1,0:T(8,128)(2,1)}, bf16[64,3584]{1,0:T(8,128)(2,1)}, u32[]{:S(2)}, u32[]{:S(2)}) collective-permute-start(bf16[64,3584]{1,0:T(8,128)(2,1)} %get-tuple-element.41), channel_id=1, source_target_pairs={{0,16},{16,32},{32,48},{48,64},{64,80},{80,96},{96,112},{112,128},... | collective-permute-start | bytes 1376264 | tf_op jit(solution)/shard_map/ppermute | solution.py:18
  168.4 39.1 %collective-permute-start.2 = (bf16[64,3584]{1,0:T(8,128)(2,1)S(1)}, bf16[64,3584]{1,0:T(8,128)(2,1)}, u32[]{:S(2)}, u32[]{:S(2)}) collective-permute-start(bf16[64,3584]{1,0:T(8,128)(2,1)S(1)} %get-tuple-element.40), channel_id=1, source_target_pairs={{16,0},{32,16},{48,32},{64,48},{80,64},{96,80},{112,96},{128,112},... | collective-permute-start | bytes 1376264 | tf_op jit(solution)/shard_map/ppermute | solution.py:20
  207.3 10.4 %slice-start = ((s8[7798784]{0:T(1024)(128)(4,1)}), s8[4194304]{0:T(1024)(128)(4,1)S(1)}, s32[]{:S(2)}) async-start(s8[7798784]{0:T(1024)(128)(4,1)} %bitcast.109), calls=%async_computation.7 | async-start | bytes 8388608
  207.5 10.3 %slice-start.1 = ((s8[7798784]{0:T(1024)(128)(4,1)}), s8[3604480]{0:T(1024)(128)(4,1)S(1)}, s32[]{:S(2)}) async-start(s8[7798784]{0:T(1024)(128)(4,1)} %bitcast.109), calls=%async_computation.8 | async-start | bytes 7208960
  272.9 210.3 %all-reduce.3.cloned.1.call-start = ((), (), s32[]{:S(2)}) async-start(), calls=%async_computation.5 | async-start | bytes 2424832 | tf_op jit(solution)/shard_map/psum | solution.py:173
  383.5 103.4 %copy-start.1 = (s32[1,272]{1,0:T(1,128)S(1)}, s32[1,272]{1,0:T(1,128)}, u32[]{:S(2)}) copy-start(s32[1,272]{1,0:T(1,128)} %param.9) | copy-start | bytes 3268
Sparse Core Ops, SparseCore 0:
  9.9 60.9 all-gather.1
  273.0 107.7 reduce-scatter.3
  384.1 99.0 all-reduce.2
